TPU v7x, 32 devices: a whole 2x2x4 slice. The times are simulated.
32 devices in a mesh: row: 8 (over z, x), col: 4 (over y, core).
Axes of the slice: x: 2, y: 2, z: 4, core: 2. Of those that a mesh axis runs over, the one named last changes fastest.
Arguments:
- hamiltonian: float32 [18432, 18432], P('row', 'col'), may hold values from -6 to 6, as said below
- panel: float32 [18432, 128], P(('row', 'col')), may hold values from -0.03125 to 0.03125
Outputs:
- updated: float32 [18432, 18432], P('row', 'col')
Inputs may be any that keep to these rules, and one draw needn't show every extreme that they name: `hamiltonian`: H is symmetric: the entry at stored row p and stored column q equals the entry whose stored row and column stand for the two global indices swapped.
All inputs are finite; a program needn't handle non-finite values.
Results may differ from a plain program's by a relative error of at most 0.0002.
Values sent between devices are 32-bit elements; how exact they have to be, the bound alone decides.
No kernel may reach another device: no remote copies, remote signals or barrier semaphores. Data moves between devices by JAX's collectives and lax.ppermute only.
A program may use at most 192 MiB of HBM per device.

v0:
```python
import jax
import jax.numpy as jnp
from jax import lax
from jax.sharding import PartitionSpec as P

B = 128
highest = lax.Precision.HIGHEST


def matmul(left, right):
    return jnp.dot(left, right, precision=highest, preferred_element_type=jnp.float32)


def shape_panel(panel_raw, global_rows, block_width):
    global_block = global_rows // block_width
    within = global_rows % block_width
    column_ids = jnp.arange(panel_raw.shape[1], dtype=jnp.int32)
    below = column_ids[None, :] < within[:, None]
    on_diagonal = column_ids[None, :] == within[:, None]
    unit_block = jnp.where(below, panel_raw, jnp.where(on_diagonal, 1.0, 0.0))
    kept = jnp.where((global_block == 1)[:, None], unit_block, 0.0)
    return jnp.where((global_block >= 2)[:, None], panel_raw, kept)


def alternate_blocks(even_rows, odd_rows, block_width):
    blocks = even_rows.shape[0] // block_width
    stacked = jnp.stack(
        [
            even_rows.reshape(blocks, block_width, even_rows.shape[1]),
            odd_rows.reshape(blocks, block_width, odd_rows.shape[1]),
        ],
        axis=1,
    )
    return stacked.reshape(2 * even_rows.shape[0], even_rows.shape[1])


def upper_inverse(gram_matrix):
    width = gram_matrix.shape[0]
    diagonal_half = jnp.diag(gram_matrix) * 0.5
    nilpotent = jnp.triu(gram_matrix, 1) / diagonal_half[:, None]
    identity_matrix = jnp.eye(width, dtype=gram_matrix.dtype)
    power = -nilpotent
    result = identity_matrix + power
    for level in range(width.bit_length()):
        power = matmul(power, power)
        result = matmul(result, identity_matrix + power)
    return result / diagonal_half[None, :]


def compact_factors(gram_matrix, cross_term):
    block_factor = upper_inverse(gram_matrix)
    middle = matmul(matmul(block_factor.T, cross_term), block_factor)
    return (block_factor, middle)


def body(hamiltonian, panel):
    rows_total = lax.axis_size("row")
    cols_total = lax.axis_size("col")
    my_row = lax.axis_index("row")
    my_col = lax.axis_index("col")
    local_rows = hamiltonian.shape[0]
    piece_rows = panel.shape[0]
    position = my_col * piece_rows + jnp.arange(piece_rows, dtype=jnp.int32)
    global_rows = (position // B * rows_total + my_row) * B + position % B
    piece = shape_panel(panel, global_rows, B)
    whole = lax.all_gather(piece, ("row", "col"), axis=0, tiled=True)
    v_rows = lax.dynamic_slice_in_dim(whole, my_row * local_rows, local_rows, 0)
    even_rows = lax.dynamic_slice_in_dim(whole, my_col * local_rows, local_rows, 0)
    odd_rows = lax.dynamic_slice_in_dim(whole, (my_col + cols_total) * local_rows, local_rows, 0)
    v_cols = alternate_blocks(even_rows, odd_rows, B)
    partial_rows = matmul(hamiltonian, v_cols)
    p_rows = lax.psum(partial_rows, "col")
    gram_part = lax.dot_general(
        v_rows,
        v_rows,
        (((0,), (0,)), ((), ())),
        precision=highest,
        preferred_element_type=jnp.float32,
    )
    cross_part = lax.dot_general(
        v_rows,
        p_rows,
        (((0,), (0,)), ((), ())),
        precision=highest,
        preferred_element_type=jnp.float32,
    )
    column_part = lax.dot_general(
        hamiltonian,
        v_rows,
        (((0,), (0,)), ((), ())),
        precision=highest,
        preferred_element_type=jnp.float32,
    )
    p_cols, gram_matrix, cross_term = lax.psum((column_part, gram_part, cross_part), "row")
    block_factor, middle = compact_factors(gram_matrix, cross_term)
    y_rows = matmul(p_rows, block_factor) - 0.5 * matmul(v_rows, middle)
    y_cols = matmul(p_cols, block_factor) - 0.5 * matmul(v_cols, middle)
    left_side = jnp.concatenate([v_rows, y_rows], axis=1)
    right_side = jnp.concatenate([y_cols, v_cols], axis=1)
    updated = hamiltonian - lax.dot_general(
        left_side,
        right_side,
        (((1,), (1,)), ((), ())),
        precision=highest,
        preferred_element_type=jnp.float32,
    )
    return updated


def solution(mesh):
    return jax.shard_map(
        body,
        mesh=mesh,
        in_specs=(P("row", "col"), P(("row", "col"), None)),
        out_specs=P("row", "col"),
        check_vma=False,
    )
```

profile of v0, /device:TPU:0, one launch (start us, length us, event | category | flops | bytes accessed | tf_op | source)
XLA Modules:
  0.0 363.7 jit_solution(16865942262701142624)
XLA Ops:
  6.5 0.0 all-gather.2.cloned.1.call-start
  6.6 2.0 select_select_fusion
  8.6 0.0 all-gather.2.cloned.1.call-update
  8.6 0.0 all-reduce.4.cloned.1.call-start
  8.6 85.8 %all-gather.2.cloned.1.call-done = f32[18432,128]{1,0:T(8,128)} async-done(((f32[576,128]{1,0:T(8,128)}), f32[18432,128]{1,0:T(8,128)}) %all-gather.2.cloned.1.call-update) | async-done | bytes 9437200 | tf_op jit(solution)/shard_map/all_gather | solution.py:66
  94.4 2.2 constant_dynamic-slice_fusion.2
  96.7 0.2 pad_maximum_fusion
  96.8 48.9 %convolution_bitcast_fusion.1 = f32[2304,128]{0,1:T(8,128)} fusion(f32[4608,128]{1,0:T(8,128)S(1)} %bitcast.51, f32[2304,4608]{1,0:T(8,128)} %param.2), kind=kOutput, calls=%fused_computation.10 | convolution fusion | flops 16307453952 | bytes 46006272 | tf_op jit(solution)/shard_map/dot_general | solution.py:11
  145.7 0.0 all-reduce.4.cloned.1.call-update
  145.7 0.5 all-reduce.6.cloned.1.call-start
  146.2 29.8 %convolution_bitcast_fusion = f32[4608,128]{0,1:T(8,128)} fusion(f32[2304,128]{1,0:T(8,128)S(1)} %get-tuple-element.8, f32[2304,4608]{1,0:T(8,128)} %param.2), kind=kOutput, calls=%fused_computation.4 | convolution fusion | flops 16307453952 | bytes 46006272 | tf_op jit(solution)/shard_map/dot_general | solution.py:87
  176.1 2.6 fusion.28
  178.7 3.3 all-reduce.4.cloned.1.call-done
  182.1 3.9 %fusion.36 = f32[128,128]{1,0:T(8,128)} fusion(f32[2304,128]{1,0:T(8,128)S(1)} %get-tuple-element.8, f32[2304,128]{0,1:T(8,128)} %all-reduce.4.cloned.1.call-done), kind=kOutput, calls=%fused_computation.79 | convolution fusion | flops 452984832 | bytes 2424832 | tf_op jit(solution)/shard_map/dot_general | solution.py:80
  186.0 0.0 all-reduce.6.cloned.1.call-update
  186.0 112.9 %all-reduce.6.cloned.1.call-done = (f32[4608,128]{0,1:T(8,128)}, f32[128,128]{1,0:T(8,128)}, f32[128,128]{1,0:T(8,128)}) async-done(((f32[4608,128]{0,1:T(8,128)}, f32[128,128]{1,0:T(8,128)}, f32[128,128]{1,0:T(8,128)}), (f32[4608,128]{0,1:T(8,128)}, f32[128,128]{1,0:T(8,128)}, f32[128,128]{1,0:T(8,128)})) %all-reduce.6.cloned.1.call-update) | async-done | bytes 2490384 | tf_op jit(solution)/shard_map/psum | solution.py:94
  298.9 1.9 gather_fusion
  300.8 0.0 copy-start.1
  300.8 1.3 fusion.27
  302.1 1.1 fusion.8
  303.2 0.2 fusion.29
  303.4 0.2 fusion.30
  303.7 0.2 fusion.9
  303.9 0.2 fusion.31
  304.1 0.2 fusion.10
  304.3 0.2 fusion.32
  304.5 0.2 fusion.11
  304.7 0.2 fusion.33
  304.9 0.2 fusion.12
  305.1 0.2 fusion.34
  305.4 0.2 fusion.13
  305.6 0.2 convolution_add_fusion
  305.8 0.2 fusion.14
  306.0 0.2 convolution_divide_fusion
  306.2 0.0 copy-done.1
  306.2 0.0 copy-start.2
  306.2 0.0 copy-start
  306.2 4.0 %fusion.39 = f32[4608,128]{1,0:T(8,128)S(1)} fusion(f32[4608,128]{0,1:T(8,128)S(1)} %copy-done.1, f32[128,128]{1,0:T(8,128)S(1)} %convolution_divide_fusion), kind=kOutput, calls=%fused_computation.82 | convolution fusion | flops 905969664 | bytes 4784128 | tf_op jit(solution)/shard_map/dot_general | solution.py:11
  310.2 0.0 copy-done.2
  310.2 0.3 fusion.37
  310.5 0.2 fusion.38
  310.7 0.0 copy-done
  310.7 2.2 fusion.35
  313.0 1.1 fusion.4
  314.1 2.1 fusion
  316.2 40.7 %convolution_subtract_fusion = f32[2304,4608]{1,0:T(8,128)} fusion(f32[2304,4608]{1,0:T(8,128)} %param.2, f32[4608,128]{1,0:T(8,128)S(1)} %bitcast.53, f32[4608,128]{1,0:T(8,128)S(1)} %fusion, f32[2304,128]{1,0:T(8,128)S(1)} %fusion.4, f32[2304,128]{1,0:T(8,128)S(1)} %get-tuple-element.8), kind=kOutput, calls=%fused_computation.1 | convolution fusion | flops 32627294208 | bytes 92012544 | tf_op jit(solution)/shard_map/dot_general | solution.py:100
  (4 shorter events, 0.1 us)
Async XLA Ops:
  6.5 87.9 %all-gather.2.cloned.1.call-start = ((), (), s32[]{:S(2)}) async-start(), calls=%async_computation | async-start | bytes 9732096 | tf_op jit(solution)/shard_map/all_gather | solution.py:66
  8.6 173.5 %all-reduce.4.cloned.1.call-start = ((), (), s32[]{:S(2)}) async-start(), calls=%async_computation.1 | async-start | bytes 2359296 | tf_op jit(solution)/shard_map/psum | solution.py:72
  145.7 153.1 %all-reduce.6.cloned.1.call-start = ((), (), s32[]{:S(2)}) async-start(), calls=%async_computation.2 | async-start | bytes 4980736 | tf_op jit(solution)/shard_map/psum | solution.py:94
  300.8 5.4 %copy-start.1 = (f32[4608,128]{0,1:T(8,128)S(1)}, f32[4608,128]{0,1:T(8,128)}, u32[]{:S(2)}) copy-start(f32[4608,128]{0,1:T(8,128)} %get-tuple-element.5) | copy-start | bytes 7077892
  306.2 4.0 %copy-start.2 = (f32[128,128]{1,0:T(8,128)S(1)}, f32[128,128]{1,0:T(8,128)}, u32[]{:S(2)}) copy-start(f32[128,128]{1,0:T(8,128)} %get-tuple-element.7) | copy-start | bytes 196612
  306.2 4.5 %copy-start = (f32[2304,128]{0,1:T(8,128)S(1)}, f32[2304,128]{0,1:T(8,128)}, u32[]{:S(2)}) copy-start(f32[2304,128]{0,1:T(8,128)} %all-reduce.4.cloned.1.call-done) | copy-start | bytes 3538948
Sparse Core Ops, SparseCore 0:
  10.2 84.1 all-gather.1
  145.8 36.1 all-reduce.3
  186.1 112.7 all-reduce.5
where the time goes:
time: 369 us; the launch traced here: 364 us
  waiting for transfers between devices  202 us (55%)
  matrix products  141 us (38%)
  between operations  13.6 us (4%)
  local copies, waits for them, and re-layouts  4.19 us (1%)
    psum x1, waiting for transfers between devices, body(): lax.psum((column_part, gram_part, cross_part), 'row')  113 us
    all_gather x1, waiting for transfers between devices, body(): whole = lax.all_gather(piece, ('row', 'col'), axis=0, tiled=True)  85.8 us
    dot_general x23, matrix products, matmul(): jnp.dot(left, right, precision=highest, preferred_element_type=jnp.float32)  64 us
    dot_general x1, matrix products, body(): lax.dot_general(left_side, right_side, (((1,), (1,)), ((), ())), precisio...  40.7 us
    dot_general x1, matrix products, body(): lax.dot_general(hamiltonian, v_rows, (((0,), (0,)), ((), ())), precision=...  29.8 us
  transfers between devices with their start and end apart: 3, of which 3 were waited for; matrix products, arithmetic and copies ran while one was open for 9% of the time, Pallas kernels for 0%

commit v1 on v0

--- a/solution.py
+++ b/solution.py
@@ -63,7 +63,10 @@
     position = my_col * piece_rows + jnp.arange(piece_rows, dtype=jnp.int32)
     global_rows = (position // B * rows_total + my_row) * B + position % B
     piece = shape_panel(panel, global_rows, B)
-    whole = lax.all_gather(piece, ("row", "col"), axis=0, tiled=True)
+    whole = jnp.concatenate(
+        lax.all_to_all(jnp.stack([piece] * lax.axis_size(("row", "col"))), ("row", "col"), 0, 0),
+        axis=0,
+    )
     v_rows = lax.dynamic_slice_in_dim(whole, my_row * local_rows, local_rows, 0)
     even_rows = lax.dynamic_slice_in_dim(whole, my_col * local_rows, local_rows, 0)
     odd_rows = lax.dynamic_slice_in_dim(whole, (my_col + cols_total) * local_rows, local_rows, 0)

time: 369 us -> 508 us (1.38)
  waiting for transfers between devices: 202 us -> 329 us
  starting transfers between devices: 0.55 us -> 7.99 us
    all_to_all x0 -> x1, waiting for transfers between devices: none -> 208 us  [body(): lax.all_to_all(jnp.stack([piece] * lax.axis_size(('row', 'col'))), ('row'...]
    all_gather x1 -> x0, waiting for transfers between devices: 85.8 us -> none  [body(): whole = lax.all_gather(piece, ('row', 'col'), axis=0, tiled=True)]
    all_to_all x0 -> x1, starting transfers between devices: none -> 7.44 us  [body(): lax.all_to_all(jnp.stack([piece] * lax.axis_size(('row', 'col'))), ('row'...]
    psum x1, waiting for transfers between devices: 3.33 us -> 8.5 us  [body(): p_rows = lax.psum(partial_rows, 'col')]
  transfers between devices with their start and end apart: 3 -> 3, of which waited for: 3 -> 3; matrix products, arithmetic and copies ran while one was open for 9% -> 6% of each run, Pallas kernels for 0% -> 0%
where the time goes in v1:
time: 508 us; the launch traced here: 502 us
  waiting for transfers between devices  329 us (65%)
  matrix products  141 us (28%)
  between operations  13.9 us (3%)
  local copies, waits for them, and re-layouts  9 us (2%)
  starting transfers between devices  7.99 us (2%)
    all_to_all x1, waiting for transfers between devices, body(): lax.all_to_all(jnp.stack([piece] * lax.axis_size(('row', 'col'))), ('row'...  208 us
    psum x1, waiting for transfers between devices, body(): lax.psum((column_part, gram_part, cross_part), 'row')  113 us
    dot_general x23, matrix products, matmul(): jnp.dot(left, right, precision=highest, preferred_element_type=jnp.float32)  63.9 us
    dot_general x1, matrix products, body(): lax.dot_general(left_side, right_side, (((1,), (1,)), ((), ())), precisio...  40.7 us
    dot_general x1, matrix products, body(): lax.dot_general(hamiltonian, v_rows, (((0,), (0,)), ((), ())), precision=...  29.6 us
  transfers between devices with their start and end apart: 3, of which 3 were waited for; matrix products, arithmetic and copies ran while one was open for 6% of the time, Pallas kernels for 0%

profile of v1, /device:TPU:0, one launch (start us, length us, event | category | flops | bytes accessed | tf_op | source)
XLA Modules:
  0.0 502.3 jit_solution(5872435452009125063)
XLA Ops:
  6.6 1.3 select_select_fusion
  7.9 4.8 stack.4
  12.7 7.4 %all-to-all-start = ((f32[32,576,128]{2,1,0:T(8,128)}), f32[32,576,128]{2,1,0:T(8,128)}, u32[]{:S(2)}, u32[]{:S(2)}) async-start(f32[32,576,128]{2,1,0:T(8,128)} %stack.4), calls=%async_computation | async-start | bytes 18874368 | tf_op jit(solution)/shard_map/all_to_all | solution.py:67
  20.1 0.0 all-reduce.4.cloned.1.call-start
  20.2 207.7 %all-to-all-done = f32[32,576,128]{2,1,0:T(8,128)} async-done(((f32[32,576,128]{2,1,0:T(8,128)}), f32[32,576,128]{2,1,0:T(8,128)}, u32[]{:S(2)}, u32[]{:S(2)}) %all-to-all-start) | async-done | bytes 9437216 | tf_op jit(solution)/shard_map/all_to_all | solution.py:67
  227.9 2.2 constant_dynamic-slice_fusion.2
  230.1 0.2 pad_maximum_fusion
  230.3 48.9 %convolution_bitcast_fusion.1 = f32[2304,128]{0,1:T(8,128)} fusion(f32[4608,128]{1,0:T(8,128)S(1)} %bitcast.52, f32[2304,4608]{1,0:T(8,128)} %param.2), kind=kOutput, calls=%fused_computation.10 | convolution fusion | flops 16307453952 | bytes 46006272 | tf_op jit(solution)/shard_map/dot_general | solution.py:11
  279.2 0.0 all-reduce.4.cloned.1.call-update
  279.2 0.5 all-reduce.6.cloned.1.call-start
  279.7 29.6 %convolution_bitcast_fusion = f32[4608,128]{0,1:T(8,128)} fusion(f32[2304,128]{1,0:T(8,128)S(1)} %get-tuple-element.8, f32[2304,4608]{1,0:T(8,128)} %param.2), kind=kOutput, calls=%fused_computation.4 | convolution fusion | flops 16307453952 | bytes 46006272 | tf_op jit(solution)/shard_map/dot_general | solution.py:90
  309.3 2.7 fusion.28
  312.0 8.5 %all-reduce.4.cloned.1.call-done = f32[2304,128]{0,1:T(8,128)} async-done(((f32[2304,128]{0,1:T(8,128)}), f32[2304,128]{0,1:T(8,128)}) %all-reduce.4.cloned.1.call-update) | async-done | bytes 1179664 | tf_op jit(solution)/shard_map/psum | solution.py:75
  320.5 3.9 fusion.36
  324.4 0.0 all-reduce.6.cloned.1.call-update
  324.4 112.9 %all-reduce.6.cloned.1.call-done = (f32[4608,128]{0,1:T(8,128)}, f32[128,128]{1,0:T(8,128)}, f32[128,128]{1,0:T(8,128)}) async-done(((f32[4608,128]{0,1:T(8,128)}, f32[128,128]{1,0:T(8,128)}, f32[128,128]{1,0:T(8,128)}), (f32[4608,128]{0,1:T(8,128)}, f32[128,128]{1,0:T(8,128)}, f32[128,128]{1,0:T(8,128)})) %all-reduce.6.cloned.1.call-update) | async-done | bytes 2490384 | tf_op jit(solution)/shard_map/psum | solution.py:97
  437.3 1.9 gather_fusion
  439.2 0.0 copy-start.1
  439.2 1.3 fusion.27
  440.5 1.1 fusion.8
  441.7 0.2 fusion.29
  441.9 0.2 fusion.30
  442.1 0.2 fusion.9
  442.3 0.2 fusion.31
  442.5 0.2 fusion.10
  442.7 0.2 fusion.32
  442.9 0.2 fusion.11
  443.1 0.2 fusion.33
  443.4 0.2 fusion.12
  443.6 0.2 fusion.34
  443.8 0.2 fusion.13
  444.0 0.2 convolution_add_fusion
  444.2 0.2 fusion.14
  444.4 0.2 convolution_divide_fusion
  444.6 0.0 copy-done.1
  444.6 0.0 copy-start.2
  444.7 0.0 copy-start
  444.7 3.8 fusion.39
  448.5 0.0 copy-done.2
  448.5 0.3 fusion.37
  448.8 0.2 fusion.38
  449.0 0.0 copy-done
  449.0 2.2 fusion.35
  451.3 1.1 fusion.4
  452.4 2.1 fusion
  454.5 40.7 %convolution_subtract_fusion = f32[2304,4608]{1,0:T(8,128)} fusion(f32[2304,4608]{1,0:T(8,128)} %param.2, f32[4608,128]{1,0:T(8,128)S(1)} %bitcast.54, f32[4608,128]{1,0:T(8,128)S(1)} %fusion, f32[2304,128]{1,0:T(8,128)S(1)} %fusion.4, f32[2304,128]{1,0:T(8,128)S(1)} %get-tuple-element.8), kind=kOutput, calls=%fused_computation.1 | convolution fusion | flops 32627294208 | bytes 92012544 | tf_op jit(solution)/shard_map/dot_general | solution.py:103
  (4 shorter events, 0.1 us)
Async XLA Ops:
  12.7 215.2 %all-to-all-start = ((f32[32,576,128]{2,1,0:T(8,128)}), f32[32,576,128]{2,1,0:T(8,128)}, u32[]{:S(2)}, u32[]{:S(2)}) async-start(f32[32,576,128]{2,1,0:T(8,128)} %stack.4), calls=%async_computation | async-start | bytes 18874368 | tf_op jit(solution)/shard_map/all_to_all | solution.py:67
  20.1 300.4 %all-reduce.4.cloned.1.call-start = ((), (), s32[]{:S(2)}) async-start(), calls=%async_computation.1 | async-start | bytes 2359296 | tf_op jit(solution)/shard_map/psum | solution.py:75
  279.2 158.1 %all-reduce.6.cloned.1.call-start = ((), (), s32[]{:S(2)}) async-start(), calls=%async_computation.2 | async-start | bytes 4980736 | tf_op jit(solution)/shard_map/psum | solution.py:97
  439.2 5.4 %copy-start.1 = (f32[4608,128]{0,1:T(8,128)S(1)}, f32[4608,128]{0,1:T(8,128)}, u32[]{:S(2)}) copy-start(f32[4608,128]{0,1:T(8,128)} %get-tuple-element.5) | copy-start | bytes 7077892
  444.6 3.9 copy-start.2
  444.7 4.4 copy-start
Sparse Core Ops, SparseCore 0:
  279.3 41.1 all-reduce.3
  324.5 112.7 all-reduce.5
